TPU v7x, 512 devices: a whole 4x4x16 slice. The times are simulated.
512 devices in a mesh: seq: 32 (over z, core), dp: 16 (over x, y).
Axes of the slice: x: 4, y: 4, z: 16, core: 2. Of those that a mesh axis runs over, the one named last changes fastest.
Arguments:
- queries: bfloat16 [16, 5120, 2048], P('dp', 'seq'), may hold values from -6 to 6
- keys: bfloat16 [16, 5120, 2048], P('dp', 'seq'), may hold values from -6 to 6
- values: bfloat16 [16, 5120, 2048], P('dp', 'seq'), may hold values from -6 to 6
- keep: int32 [16, 5120, 2048], P('dp', 'seq'), may hold values 0 or 1
- gain: float32 [2048], replicated, may hold values from 0.25 to 1.75
- out_weight: bfloat16 [2048, 2048], P(None, 'dp'), may hold values from -0.125 to 0.125
Outputs:
- projected: bfloat16 [16, 5120, 2048], P('dp', 'seq')
All inputs are finite; a program needn't handle non-finite values. No bound on the sum of `keep` on one device may be relied on, other than what follows from the above.
Results may differ from a plain program's by a relative error of at most 0.0051.
Values may be sent and summed in bfloat16 or wider, within the bound.
No kernel may reach another device: no remote copies, remote signals or barrier semaphores. Data moves between devices by JAX's collectives and lax.ppermute only.
A program may use at most 128 MiB of HBM per device.

v0:
```python
import jax
import jax.numpy as jnp
from jax import lax
from jax.sharding import PartitionSpec as P

HEADS = 16
HEAD = 128


def prefix_2(x, axis, combine, identity):
    size, place = (lax.axis_size(axis), lax.axis_index(axis))
    everything = lax.all_gather(x, axis)
    start = jnp.broadcast_to(jnp.asarray(identity, x.dtype), x.shape)

    def turn(k, before):
        reached = k < place
        new = combine(before, everything[k])
        return jnp.where(reached, new, before)

    return lax.fori_loop(0, size, turn, start)


def feature(x):
    xf = x.astype(jnp.float32)
    return jnp.where(xf > 0, xf + 1.0, jnp.exp(jnp.minimum(xf, 0.0))).astype(jnp.bfloat16)


def add_states(earlier, later):
    return earlier + later


def on_device(queries, keys, values, keep, gain, out_weight):
    tok_rows = queries.shape[1]
    fq = feature(queries[0]).reshape(tok_rows, HEADS, HEAD)
    fk = feature(keys[0]).reshape(tok_rows, HEADS, HEAD)
    vals = values[0].reshape(tok_rows, HEADS, HEAD)
    state = jnp.einsum("thc,thd->hcd", fk, vals, preferred_element_type=jnp.float32)
    prefix = prefix_2(state, "seq", add_states, jnp.zeros_like(state))
    prefix = prefix.astype(jnp.bfloat16)
    inter = jnp.einsum("thc,hcd->thd", fq, prefix, preferred_element_type=jnp.float32)
    causal = jnp.arange(tok_rows)[:, None] >= jnp.arange(tok_rows)[None, :]
    scores = jnp.einsum("thc,shc->hts", fq, fk, preferred_element_type=jnp.float32)
    scores = jnp.where(causal[None], scores, 0.0).astype(jnp.bfloat16)
    intra = jnp.einsum("hts,shd->thd", scores, vals, preferred_element_type=jnp.float32)
    numer = inter + intra
    normed = (
        numer
        * lax.rsqrt(jnp.mean(numer * numer, axis=-1, keepdims=True) + 1e-06)
        * gain.reshape(HEADS, HEAD)
    )
    mask = keep[0].reshape(tok_rows, HEADS, HEAD).astype(jnp.float32)
    dropped = (normed * mask * (1.0 / 0.9)).astype(jnp.bfloat16).reshape(tok_rows, HEADS * HEAD)
    result = jnp.dot(
        dropped,
        lax.all_gather(out_weight, "dp", axis=1, tiled=True),
        preferred_element_type=jnp.float32,
    ).astype(jnp.bfloat16)
    return result[None]


def solution(mesh):
    return jax.shard_map(
        on_device,
        mesh=mesh,
        in_specs=(
            P("dp", "seq", None),
            P("dp", "seq", None),
            P("dp", "seq", None),
            P("dp", "seq", None),
            P(),
            P(None, "dp"),
        ),
        out_specs=P("dp", "seq", None),
        check_vma=False,
    )
```

profile of v0, /device:TPU:2, one launch (start us, length us, event | category | flops | bytes accessed | tf_op | source)
XLA Modules:
  0.0 313.0 jit_solution(7465845264773032418)
XLA Ops:
  6.5 0.0 copy-start.3
  6.5 0.0 all-gather.6.cloned.1.call-start
  6.5 1.5 fusion.16
  8.0 0.1 copy.27
  8.2 0.0 copy-done.3
  8.2 0.1 copy.28
  8.3 0.0 copy-start
  8.3 0.8 copy-done
  9.2 1.5 fusion.23
  10.7 0.0 all-gather.6.cloned.1.call-update
  10.7 0.0 all-gather.4.cloned.1.call-start
  10.8 0.7 all-gather.4.cloned.1.call-update
  11.5 0.0 copy-start.2
  11.5 1.5 fusion.15
  13.0 1.0 copy.26
  14.0 0.0 copy-done.2
  14.0 0.1 convert_bitcast_fusion
  14.1 0.2 copy.29
  14.4 3.3 %fusion.3 = f32[160,16,128]{2,0,1:T(8,128)} fusion(pred[160,160]{1,0:T(8,128)(4,1)S(1)} %iota_compare_fusion, bf16[160,16,128]{2,1,0:T(8,128)(2,1)} %bitcast.42, bf16[160,16,128]{2,1,0:T(8,128)(2,1)} %bitcast.41, bf16[160,16,128]{2,1,0:T(8,128)(2,1)S(1)} %bitcast.39), kind=kOutput, calls=%fused_computation.13 | convolution fusion | flops 210534400 | bytes 3302400 | tf_op jit(solution)/shard_map/hts,shd->thd/dot_general | solution.py:44
  17.7 188.8 %all-gather.6.cloned.1.call-done = f32[512,128,128]{2,1,0:T(8,128)} async-done(((f32[16,128,128]{2,1,0:T(8,128)}), f32[512,128,128]{2,1,0:T(8,128)}) %all-gather.6.cloned.1.call-update) | async-done | bytes 33554448 | tf_op jit(solution)/shard_map/all_gather | solution.py:12
  206.5 0.0 copy-start.1
  206.5 51.9 %while.14 = (s32[]{:T(128)}, f32[16,128,128]{2,1,0:T(8,128)S(1)}, s32[]{:T(128)}, f32[32,16,128,128]{3,2,1,0:T(8,128)}, s32[]{:T(128)}, /*index=5*/s32[]{:T(128)}) while((s32[]{:T(128)}, f32[16,128,128]{2,1,0:T(8,128)S(1)}, s32[]{:T(128)}, f32[32,16,128,128]{3,2,1,0:T(8,128)}, s32[]{:T(128)}, /*index=5*/s32[]{:T(128)}) %tuple.40), condition=%wide.region_1.2_spmd.clone, body=%wide.region_0.1_spmd.clone.sunk | while | flops 786436 | bytes 3145821 | solution.py:20
  206.5 1.7 add_select_fusion.2
  208.2 1.6 add_select_fusion.2
  209.8 1.6 add_select_fusion.2
  211.4 1.6 add_select_fusion.2
  213.0 1.6 add_select_fusion.2
  214.6 1.6 add_select_fusion.2
  216.2 1.6 add_select_fusion.2
  217.8 1.6 add_select_fusion.2
  219.5 1.6 add_select_fusion.2
  221.1 1.6 add_select_fusion.2
  222.7 1.6 add_select_fusion.2
  224.3 1.7 add_select_fusion.2
  226.0 1.6 add_select_fusion.2
  227.7 1.6 add_select_fusion.2
  229.3 1.6 add_select_fusion.2
  230.9 1.6 add_select_fusion.2
  232.5 1.6 add_select_fusion.2
  234.1 1.6 add_select_fusion.2
  235.8 1.6 add_select_fusion.2
  237.4 1.6 add_select_fusion.2
  239.0 1.6 add_select_fusion.2
  240.6 1.6 add_select_fusion.2
  242.2 1.6 add_select_fusion.2
  243.9 1.6 add_select_fusion.2
  245.5 1.6 add_select_fusion.2
  247.1 1.6 add_select_fusion.2
  248.7 1.6 add_select_fusion.2
  250.3 1.6 add_select_fusion.2
  251.9 1.6 add_select_fusion.2
  253.5 1.6 add_select_fusion.2
  255.2 1.6 add_select_fusion.2
  256.8 1.6 add_select_fusion.2
  258.4 0.0 copy-done.1
  258.4 0.0 copy-start.4
  258.4 3.1 multiply_reduce_fusion
  261.5 38.1 %all-gather.4.cloned.1.call-done = bf16[2048,2048]{1,0:T(8,128)(2,1)} async-done(((bf16[2048,128]{1,0:T(8,128)(2,1)}), bf16[2048,2048]{1,0:T(8,128)(2,1)}) %all-gather.4.cloned.1.call-update) | async-done | bytes 8388624 | tf_op jit(solution)/shard_map/all_gather | solution.py:55
  299.6 0.0 copy-done.4
  299.6 6.6 %fusion = bf16[1,160,2048]{2,1,0:T(8,128)(2,1)} fusion(bf16[2048,2048]{1,0:T(8,128)(2,1)} %all-gather.4.cloned.1.call-done, f32[160,16,128]{2,1,0:T(8,128)S(1)} %bitcast.37, f32[160,16,128]{2,0,1:T(8,128)} %get-tuple-element.109, f32[16,128]{1,0:T(8,128)S(1)} %bitcast.46, f32[160,16]{0,1:T(8,128)S(1)} %add_rsqrt_fusion), kind=kOutput, calls=%fused_computation.3 | convolution fusion | flops 1344143360 | bytes 11683840 | tf_op jit(solution)/shard_map/dot_general | solution.py:53
  (3 shorter events, 0.0 us)
Async XLA Ops:
  6.5 1.6 copy-start.3
  6.5 199.9 %all-gather.6.cloned.1.call-start = ((), (), s32[]{:S(2)}) async-start(), calls=%async_computation.1 | async-start | bytes 34603008 | tf_op jit(solution)/shard_map/all_gather | solution.py:12
  8.3 0.9 copy-start
  10.7 288.9 %all-gather.4.cloned.1.call-start = ((), (), s32[]{:S(2)}) async-start(), calls=%async_computation | async-start | bytes 8912896 | tf_op jit(solution)/shard_map/all_gather | solution.py:55
  11.5 2.5 copy-start.2
  206.5 51.9 %copy-start.1 = (bf16[20,8,16,128]{3,2,1,0:T(8,128)(2,1)S(1)}, bf16[20,8,16,128]{3,2,1,0:T(8,128)(2,1)}, u32[]{:S(2)}) copy-start(bf16[20,8,16,128]{3,2,1,0:T(8,128)(2,1)} %copy.26) | copy-start | bytes 1966084
  258.4 41.2 %copy-start.4 = (f32[2048]{0:T(1024)S(1)}, f32[2048]{0:T(1024)}, u32[]{:S(2)}) copy-start(f32[2048]{0:T(1024)} %param.12) | copy-start | bytes 24580
Sparse Core Ops, SparseCore 0:
  10.8 195.6 all-gather.5
  209.5 90.0 all-gather.3
where the time goes:
time: 314 us; the launch traced here: 313 us
  waiting for transfers between devices  228 us (73%)
  other arithmetic  54.3 us (17%)
  matrix products  14.4 us (5%)
  between operations  13.5 us (4%)
    all_gather x1, waiting for transfers between devices, prefix_2(): everything = lax.all_gather(x, axis)  189 us
    select_n x32, other arithmetic, turn(): return jnp.where(reached, new, before)  51.1 us
    all_gather x1, waiting for transfers between devices, on_device(): lax.all_gather(out_weight, 'dp', axis=1, tiled=True)  38.1 us
    dot_general x1, matrix products, on_device(): jnp.dot(dropped, lax.all_gather(out_weight, 'dp', axis=1, tiled=True), pr...  6.56 us
  transfers between devices with their start and end apart: 2, of which 2 were waited for; matrix products, arithmetic and copies ran while one was open for 19% of the time, Pallas kernels for 0%

commit v1 on v0

--- a/solution.py
+++ b/solution.py
@@ -5,6 +5,24 @@
 
 HEADS = 16
 HEAD = 128
+
+
+def collect(shard, axis, dim):
+    ways, here, turn = (lax.axis_size(axis), lax.axis_index(axis), shard.shape[dim])
+    shape = [n * ways if d == dim else n for d, n in enumerate(shard.shape)]
+    full = lax.dynamic_update_slice_in_dim(
+        jnp.zeros(shape, shard.dtype), shard, here * turn, axis=dim
+    )
+    going_up = going_down = shard
+    for far in range(1, ways // 2 + 1):
+        going_up = lax.ppermute(going_up, axis, [(d, (d + 1) % ways) for d in range(ways)])
+        full = lax.dynamic_update_slice_in_dim(full, going_up, (here - far) % ways * turn, axis=dim)
+        if 2 * far < ways:
+            going_down = lax.ppermute(going_down, axis, [(d, (d - 1) % ways) for d in range(ways)])
+            full = lax.dynamic_update_slice_in_dim(
+                full, going_down, (here + far) % ways * turn, axis=dim
+            )
+    return full
 
 
 def prefix_2(x, axis, combine, identity):
@@ -51,9 +69,7 @@
     mask = keep[0].reshape(tok_rows, HEADS, HEAD).astype(jnp.float32)
     dropped = (normed * mask * (1.0 / 0.9)).astype(jnp.bfloat16).reshape(tok_rows, HEADS * HEAD)
     result = jnp.dot(
-        dropped,
-        lax.all_gather(out_weight, "dp", axis=1, tiled=True),
-        preferred_element_type=jnp.float32,
+        dropped, collect(out_weight, "dp", 1), preferred_element_type=jnp.float32
     ).astype(jnp.bfloat16)
     return result[None]
 

time: 314 us -> 277 us (0.88)
  the two profiles are of different devices: /device:TPU:2 before, /device:TPU:1 now
where the time goes in v1:
time: 277 us; the launch traced here: 275 us
  waiting for transfers between devices  100 us (36%)
  starting transfers between devices  65.5 us (24%)
  other arithmetic  55 us (20%)
  local copies, waits for them, and re-layouts  27.8 us (10%)
  between operations  13.7 us (5%)
  matrix products  11.7 us (4%)
    all_gather x1, waiting for transfers between devices, prefix_2(): everything = lax.all_gather(x, axis)  75.6 us
    select_n x32, other arithmetic, turn(): return jnp.where(reached, new, before)  50.9 us
    ppermute x7, starting transfers between devices, collect(): lax.ppermute(going_down, axis, [(d, (d - 1) % ways) for d in range(ways)])  45.1 us
    ppermute x8, waiting for transfers between devices, collect(): lax.ppermute(going_up, axis, [(d, (d + 1) % ways) for d in range(ways)])  20.7 us
    ppermute x8, starting transfers between devices, collect(): lax.ppermute(going_up, axis, [(d, (d + 1) % ways) for d in range(ways)])  20.4 us
    dynamic_update_slice x8, local copies, waits for them, and re-layouts, collect(): lax.dynamic_update_slice_in_dim(full, going_up, (here - far) % ways * tur...  11.4 us
    dynamic_update_slice x7, local copies, waits for them, and re-layouts, collect(): lax.dynamic_update_slice_in_dim(full, going_down, (here + far) % ways * t...  8.26 us
    dot_general x1, matrix products, on_device(): jnp.dot(dropped, collect(out_weight, 'dp', 1), preferred_element_type=jnp...  6.16 us
  transfers between devices with their start and end apart: 16, of which 9 were waited for; matrix products, arithmetic and copies ran while one was open for 11% of the time, Pallas kernels for 0%

profile of v1, /device:TPU:1, one launch (start us, length us, event | category | flops | bytes accessed | tf_op | source)
XLA Modules:
  0.0 274.8 jit_solution(17946082432777871720)
XLA Ops:
  11.0 4.0 %collective-permute-start = (bf16[2048,128]{1,0:T(8,128)(2,1)}, bf16[2048,128]{1,0:T(8,128)(2,1)S(1)}, u32[]{:S(2)}, u32[]{:S(2)}) collective-permute-start(bf16[2048,128]{1,0:T(8,128)(2,1)} %param.13), channel_id=1, source_target_pairs={{0,1},{1,2},{2,3},{3,4},{4,5},{5,6},{6,7},{7,8},{8,9},{9,10},{10,1... | collective-permute-start | bytes 1572872 | tf_op jit(solution)/shard_map/ppermute | solution.py:18
  15.0 5.6 %collective-permute-start.1 = (bf16[2048,128]{1,0:T(8,128)(2,1)}, bf16[2048,128]{1,0:T(8,128)(2,1)}, u32[]{:S(2)}, u32[]{:S(2)}) collective-permute-start(bf16[2048,128]{1,0:T(8,128)(2,1)} %param.13), channel_id=1, source_target_pairs={{0,15},{1,0},{2,1},{3,2},{4,3},{5,4},{6,5},{7,6},{8,7},{9,8},{10,9... | collective-permute-start | bytes 1572872 | tf_op jit(solution)/shard_map/ppermute | solution.py:21
  20.6 4.8 %collective-permute-done = bf16[2048,128]{1,0:T(8,128)(2,1)S(1)} collective-permute-done((bf16[2048,128]{1,0:T(8,128)(2,1)}, bf16[2048,128]{1,0:T(8,128)(2,1)S(1)}, u32[]{:S(2)}, u32[]{:S(2)}) %collective-permute-start) | collective-permute-done | bytes 524320 | tf_op jit(solution)/shard_map/ppermute | solution.py:18
  25.4 3.7 %collective-permute-start.2 = (bf16[2048,128]{1,0:T(8,128)(2,1)S(1)}, bf16[2048,128]{1,0:T(8,128)(2,1)}, u32[]{:S(2)}, u32[]{:S(2)}) collective-permute-start(bf16[2048,128]{1,0:T(8,128)(2,1)S(1)} %collective-permute-done), channel_id=1, source_target_pairs={{0,1},{1,2},{2,3},{3,4},{4,5},{5,6},{6,7},{7,8},{8,9},{9,10},{10,1... | collective-permute-start | bytes 1572872 | tf_op jit(solution)/shard_map/ppermute | solution.py:18
  29.1 6.3 %collective-permute-start.3 = (bf16[2048,128]{1,0:T(8,128)(2,1)}, bf16[2048,128]{1,0:T(8,128)(2,1)}, u32[]{:S(2)}, u32[]{:S(2)}) collective-permute-start(bf16[2048,128]{1,0:T(8,128)(2,1)} %collective-permute-done.1), channel_id=1, source_target_pairs={{0,15},{1,0},{2,1},{3,2},{4,3},{5,4},{6,5},{7,6},{8,7},{9,8},{10,9... | collective-permute-start | bytes 1572872 | tf_op jit(solution)/shard_map/ppermute | solution.py:21
  37.1 3.1 %collective-permute-done.2 = bf16[2048,128]{1,0:T(8,128)(2,1)} collective-permute-done((bf16[2048,128]{1,0:T(8,128)(2,1)S(1)}, bf16[2048,128]{1,0:T(8,128)(2,1)}, u32[]{:S(2)}, u32[]{:S(2)}) %collective-permute-start.2) | collective-permute-done | bytes 524320 | tf_op jit(solution)/shard_map/ppermute | solution.py:18
  40.2 2.8 %collective-permute-start.4 = (bf16[2048,128]{1,0:T(8,128)(2,1)}, bf16[2048,128]{1,0:T(8,128)(2,1)}, u32[]{:S(2)}, u32[]{:S(2)}) collective-permute-start(bf16[2048,128]{1,0:T(8,128)(2,1)} %collective-permute-done.2), channel_id=1, source_target_pairs={{0,1},{1,2},{2,3},{3,4},{4,5},{5,6},{6,7},{7,8},{8,9},{9,10},{10,1... | collective-permute-start | bytes 1572872 | tf_op jit(solution)/shard_map/ppermute | solution.py:18
  43.0 2.0 fusion.3
  45.0 6.5 %collective-permute-start.5 = (bf16[2048,128]{1,0:T(8,128)(2,1)}, bf16[2048,128]{1,0:T(8,128)(2,1)S(1)}, u32[]{:S(2)}, u32[]{:S(2)}) collective-permute-start(bf16[2048,128]{1,0:T(8,128)(2,1)} %collective-permute-done.3), channel_id=1, source_target_pairs={{0,15},{1,0},{2,1},{3,2},{4,3},{5,4},{6,5},{7,6},{8,7},{9,8},{10,9... | collective-permute-start | bytes 1572872 | tf_op jit(solution)/shard_map/ppermute | solution.py:21
  52.6 1.7 collective-permute-done.4
  54.3 2.2 collective-permute-start.6
  56.5 4.3 %broadcast_in_dim.28 = bf16[2048,2048]{1,0:T(8,128)(2,1)} broadcast(bf16[]{:T(256)} %constant.130.clone.1), dimensions={} | broadcast | bytes 8388610 | tf_op jit(solution)/shard_map/broadcast_in_dim | solution.py:14
  63.3 2.0 constant_dynamic-update-slice_fusion.14
  65.3 6.4 %collective-permute-start.7 = (bf16[2048,128]{1,0:T(8,128)(2,1)S(1)}, bf16[2048,128]{1,0:T(8,128)(2,1)S(1)}, u32[]{:S(2)}, u32[]{:S(2)}) collective-permute-start(bf16[2048,128]{1,0:T(8,128)(2,1)S(1)} %collective-permute-done.5), channel_id=1, source_target_pairs={{0,15},{1,0},{2,1},{3,2},{4,3},{5,4},{6,5},{7,6},{8,7},{9,8},{10,9... | collective-permute-start | bytes 1572872 | tf_op jit(solution)/shard_map/ppermute | solution.py:21
  71.7 1.9 constant_dynamic-update-slice_fusion.13
  73.7 1.9 collective-permute-start.8
  75.6 1.9 constant_dynamic-update-slice_fusion.12
  77.5 1.9 constant_dynamic-update-slice_fusion.11
  79.4 6.6 %collective-permute-start.9 = (bf16[2048,128]{1,0:T(8,128)(2,1)S(1)}, bf16[2048,128]{1,0:T(8,128)(2,1)S(1)}, u32[]{:S(2)}, u32[]{:S(2)}) collective-permute-start(bf16[2048,128]{1,0:T(8,128)(2,1)S(1)} %collective-permute-done.7), channel_id=1, source_target_pairs={{0,15},{1,0},{2,1},{3,2},{4,3},{5,4},{6,5},{7,6},{8,7},{9,8},{10,9... | collective-permute-start | bytes 1572872 | tf_op jit(solution)/shard_map/ppermute | solution.py:21
  86.1 1.9 constant_dynamic-update-slice_fusion.10
  88.0 1.9 collective-permute-start.10
  90.8 2.0 constant_dynamic-update-slice_fusion.8
  92.8 6.6 %collective-permute-start.11 = (bf16[2048,128]{1,0:T(8,128)(2,1)S(1)}, bf16[2048,128]{1,0:T(8,128)(2,1)S(1)}, u32[]{:S(2)}, u32[]{:S(2)}) collective-permute-start(bf16[2048,128]{1,0:T(8,128)(2,1)S(1)} %collective-permute-done.9), channel_id=1, source_target_pairs={{0,15},{1,0},{2,1},{3,2},{4,3},{5,4},{6,5},{7,6},{8,7},{9,8},{10,9... | collective-permute-start | bytes 1572872 | tf_op jit(solution)/shard_map/ppermute | solution.py:21
  101.2 1.9 collective-permute-start.12
  106.4 7.1 %collective-permute-start.13 = (bf16[2048,128]{1,0:T(8,128)(2,1)S(1)}, bf16[2048,128]{1,0:T(8,128)(2,1)S(1)}, u32[]{:S(2)}, u32[]{:S(2)}) collective-permute-start(bf16[2048,128]{1,0:T(8,128)(2,1)S(1)} %collective-permute-done.11), channel_id=1, source_target_pairs={{0,15},{1,0},{2,1},{3,2},{4,3},{5,4},{6,5},{7,6},{8,7},{9,8},{10,9... | collective-permute-start | bytes 1572872 | tf_op jit(solution)/shard_map/ppermute | solution.py:21
  115.7 1.9 collective-permute-start.14
  119.4 2.4 collective-permute-done.13
  122.6 8.8 %collective-permute-done.14 = bf16[2048,128]{1,0:T(8,128)(2,1)S(1)} collective-permute-done((bf16[2048,128]{1,0:T(8,128)(2,1)S(1)}, bf16[2048,128]{1,0:T(8,128)(2,1)S(1)}, u32[]{:S(2)}, u32[]{:S(2)}) %collective-permute-start.14) | collective-permute-done | bytes 524320 | tf_op jit(solution)/shard_map/ppermute | solution.py:18
  132.4 75.6 %all-gather.3.cloned.1.call-done = f32[512,128,128]{2,1,0:T(8,128)} async-done(((f32[16,128,128]{2,1,0:T(8,128)}), f32[512,128,128]{2,1,0:T(8,128)}) %all-gather.3.cloned.1.call-update) | async-done | bytes 33554448 | tf_op jit(solution)/shard_map/all_gather | solution.py:30
  208.0 51.6 %while.14 = (s32[]{:T(128)}, f32[16,128,128]{2,1,0:T(8,128)S(1)}, s32[]{:T(128)}, f32[32,16,128,128]{3,2,1,0:T(8,128)}, s32[]{:T(128)}, /*index=5*/s32[]{:T(128)}) while((s32[]{:T(128)}, f32[16,128,128]{2,1,0:T(8,128)S(1)}, s32[]{:T(128)}, f32[32,16,128,128]{3,2,1,0:T(8,128)}, s32[]{:T(128)}, /*index=5*/s32[]{:T(128)}) %tuple.38), condition=%wide.region_1.2_spmd.clone, body=%wide.region_0.1_spmd.clone.sunk | while | flops 786436 | bytes 3145821 | solution.py:38
  208.0 1.6 add_select_fusion.2
  209.6 1.6 add_select_fusion.2
  211.2 1.6 add_select_fusion.2
  212.8 1.6 add_select_fusion.2
  214.5 1.6 add_select_fusion.2
  216.1 1.6 add_select_fusion.2
  217.7 1.6 add_select_fusion.2
  219.3 1.6 add_select_fusion.2
  220.9 1.6 add_select_fusion.2
  222.5 1.6 add_select_fusion.2
  224.1 1.6 add_select_fusion.2
  225.8 1.6 add_select_fusion.2
  227.4 1.6 add_select_fusion.2
  229.0 1.6 add_select_fusion.2
  230.6 1.6 add_select_fusion.2
  232.2 1.6 add_select_fusion.2
  233.8 1.6 add_select_fusion.2
  235.4 1.6 add_select_fusion.2
  237.0 1.6 add_select_fusion.2
  238.7 1.6 add_select_fusion.2
  240.3 1.6 add_select_fusion.2
  241.9 1.6 add_select_fusion.2
  243.5 1.6 add_select_fusion.2
  245.1 1.6 add_select_fusion.2
  246.7 1.6 add_select_fusion.2
  248.3 1.6 add_select_fusion.2
  250.0 1.6 add_select_fusion.2
  251.6 1.6 add_select_fusion.2
  253.2 1.6 add_select_fusion.2
  254.8 1.6 add_select_fusion.2
  256.4 1.6 add_select_fusion.2
  258.0 1.6 add_select_fusion.2
  259.6 2.1 multiply_reduce_fusion
  261.8 6.2 %fusion = bf16[1,160,2048]{2,1,0:T(8,128)(2,1)} fusion(bf16[2048,2048]{1,0:T(8,128)(2,1)} %constant_dynamic-update-slice_fusion, f32[160,16,128]{2,1,0:T(8,128)S(1)} %bitcast.37, f32[160,16,128]{2,0,1:T(8,128)S(1)} %get-tuple-element.109, f32[16,128]{1,0:T(8,128)S(1)} %bitcast.46, f32[160,16]{0,1:T(8,128)S(1)} %add_rsqrt_fusion), kind=kOutput, calls=%fused_computation.3 | convolution fusion | flops 1344143360 | bytes 11683840 | tf_op jit(solution)/shard_map/dot_general | solution.py:71
  (41 shorter events, 21.3 us)
Async XLA Ops:
  6.5 44.9 %copy-start = (s32[1,160,2048]{2,1,0:T(8,128)S(1)}, s32[1,160,2048]{2,1,0:T(8,128)}, u32[]{:S(2)}) copy-start(s32[1,160,2048]{2,1,0:T(8,128)} %param.11) | copy-start | bytes 3932164
  6.5 201.5 %all-gather.3.cloned.1.call-start = ((), (), s32[]{:S(2)}) async-start(), calls=%async_computation | async-start | bytes 34603008 | tf_op jit(solution)/shard_map/all_gather | solution.py:30
  11.0 14.4 %collective-permute-start = (bf16[2048,128]{1,0:T(8,128)(2,1)}, bf16[2048,128]{1,0:T(8,128)(2,1)S(1)}, u32[]{:S(2)}, u32[]{:S(2)}) collective-permute-start(bf16[2048,128]{1,0:T(8,128)(2,1)} %param.13), channel_id=1, source_target_pairs={{0,1},{1,2},{2,3},{3,4},{4,5},{5,6},{6,7},{7,8},{8,9},{9,10},{10,1... | collective-permute-start | bytes 1572872 | tf_op jit(solution)/shard_map/ppermute | solution.py:18
  15.0 14.1 %collective-permute-start.1 = (bf16[2048,128]{1,0:T(8,128)(2,1)}, bf16[2048,128]{1,0:T(8,128)(2,1)}, u32[]{:S(2)}, u32[]{:S(2)}) collective-permute-start(bf16[2048,128]{1,0:T(8,128)(2,1)} %param.13), channel_id=1, source_target_pairs={{0,15},{1,0},{2,1},{3,2},{4,3},{5,4},{6,5},{7,6},{8,7},{9,8},{10,9... | collective-permute-start | bytes 1572872 | tf_op jit(solution)/shard_map/ppermute | solution.py:21
  25.4 11.7 %copy-start.2 = (bf16[2048,128]{1,0:T(8,128)(2,1)}, bf16[2048,128]{1,0:T(8,128)(2,1)S(1)}, u32[]{:S(2)}) copy-start(bf16[2048,128]{1,0:T(8,128)(2,1)S(1)} %collective-permute-done) | copy-start | bytes 1572868
  25.4 14.8 %collective-permute-start.2 = (bf16[2048,128]{1,0:T(8,128)(2,1)S(1)}, bf16[2048,128]{1,0:T(8,128)(2,1)}, u32[]{:S(2)}, u32[]{:S(2)}) collective-permute-start(bf16[2048,128]{1,0:T(8,128)(2,1)S(1)} %collective-permute-done), channel_id=1, source_target_pairs={{0,1},{1,2},{2,3},{3,4},{4,5},{5,6},{6,7},{7,8},{8,9},{9,10},{10,1... | collective-permute-start | bytes 1572872 | tf_op jit(solution)/shard_map/ppermute | solution.py:18
  29.1 15.9 %collective-permute-start.3 = (bf16[2048,128]{1,0:T(8,128)(2,1)}, bf16[2048,128]{1,0:T(8,128)(2,1)}, u32[]{:S(2)}, u32[]{:S(2)}) collective-permute-start(bf16[2048,128]{1,0:T(8,128)(2,1)} %collective-permute-done.1), channel_id=1, source_target_pairs={{0,15},{1,0},{2,1},{3,2},{4,3},{5,4},{6,5},{7,6},{8,7},{9,8},{10,9... | collective-permute-start | bytes 1572872 | tf_op jit(solution)/shard_map/ppermute | solution.py:21
  40.2 14.1 %collective-permute-start.4 = (bf16[2048,128]{1,0:T(8,128)(2,1)}, bf16[2048,128]{1,0:T(8,128)(2,1)}, u32[]{:S(2)}, u32[]{:S(2)}) collective-permute-start(bf16[2048,128]{1,0:T(8,128)(2,1)} %collective-permute-done.2), channel_id=1, source_target_pairs={{0,1},{1,2},{2,3},{3,4},{4,5},{5,6},{6,7},{7,8},{8,9},{9,10},{10,1... | collective-permute-start | bytes 1572872 | tf_op jit(solution)/shard_map/ppermute | solution.py:18
  45.0 15.9 %copy-start.1 = (bf16[2048,128]{1,0:T(8,128)(2,1)S(1)}, bf16[2048,128]{1,0:T(8,128)(2,1)}, u32[]{:S(2)}) copy-start(bf16[2048,128]{1,0:T(8,128)(2,1)} %param.13) | copy-start | bytes 1572868
  45.0 20.3 %collective-permute-start.5 = (bf16[2048,128]{1,0:T(8,128)(2,1)}, bf16[2048,128]{1,0:T(8,128)(2,1)S(1)}, u32[]{:S(2)}, u32[]{:S(2)}) collective-permute-start(bf16[2048,128]{1,0:T(8,128)(2,1)} %collective-permute-done.3), channel_id=1, source_target_pairs={{0,15},{1,0},{2,1},{3,2},{4,3},{5,4},{6,5},{7,6},{8,7},{9,8},{10,9... | collective-permute-start | bytes 1572872 | tf_op jit(solution)/shard_map/ppermute | solution.py:21
  54.3 19.3 %collective-permute-start.6 = (bf16[2048,128]{1,0:T(8,128)(2,1)}, bf16[2048,128]{1,0:T(8,128)(2,1)}, u32[]{:S(2)}, u32[]{:S(2)}) collective-permute-start(bf16[2048,128]{1,0:T(8,128)(2,1)} %collective-permute-done.4), channel_id=1, source_target_pairs={{0,1},{1,2},{2,3},{3,4},{4,5},{5,6},{6,7},{7,8},{8,9},{9,10},{10,1... | collective-permute-start | bytes 1572872 | tf_op jit(solution)/shard_map/ppermute | solution.py:18
  65.3 14.1 %collective-permute-start.7 = (bf16[2048,128]{1,0:T(8,128)(2,1)S(1)}, bf16[2048,128]{1,0:T(8,128)(2,1)S(1)}, u32[]{:S(2)}, u32[]{:S(2)}) collective-permute-start(bf16[2048,128]{1,0:T(8,128)(2,1)S(1)} %collective-permute-done.5), channel_id=1, source_target_pairs={{0,15},{1,0},{2,1},{3,2},{4,3},{5,4},{6,5},{7,6},{8,7},{9,8},{10,9... | collective-permute-start | bytes 1572872 | tf_op jit(solution)/shard_map/ppermute | solution.py:21
  73.7 14.3 %collective-permute-start.8 = (bf16[2048,128]{1,0:T(8,128)(2,1)}, bf16[2048,128]{1,0:T(8,128)(2,1)S(1)}, u32[]{:S(2)}, u32[]{:S(2)}) collective-permute-start(bf16[2048,128]{1,0:T(8,128)(2,1)} %collective-permute-done.6), channel_id=1, source_target_pairs={{0,1},{1,2},{2,3},{3,4},{4,5},{5,6},{6,7},{7,8},{8,9},{9,10},{10,1... | collective-permute-start | bytes 1572872 | tf_op jit(solution)/shard_map/ppermute | solution.py:18
  79.4 13.4 %collective-permute-start.9 = (bf16[2048,128]{1,0:T(8,128)(2,1)S(1)}, bf16[2048,128]{1,0:T(8,128)(2,1)S(1)}, u32[]{:S(2)}, u32[]{:S(2)}) collective-permute-start(bf16[2048,128]{1,0:T(8,128)(2,1)S(1)} %collective-permute-done.7), channel_id=1, source_target_pairs={{0,15},{1,0},{2,1},{3,2},{4,3},{5,4},{6,5},{7,6},{8,7},{9,8},{10,9... | collective-permute-start | bytes 1572872 | tf_op jit(solution)/shard_map/ppermute | solution.py:21
  88.0 13.2 %collective-permute-start.10 = (bf16[2048,128]{1,0:T(8,128)(2,1)S(1)}, bf16[2048,128]{1,0:T(8,128)(2,1)S(1)}, u32[]{:S(2)}, u32[]{:S(2)}) collective-permute-start(bf16[2048,128]{1,0:T(8,128)(2,1)S(1)} %collective-permute-done.8), channel_id=1, source_target_pairs={{0,1},{1,2},{2,3},{3,4},{4,5},{5,6},{6,7},{7,8},{8,9},{9,10},{10,1... | collective-permute-start | bytes 1572872 | tf_op jit(solution)/shard_map/ppermute | solution.py:18
  92.8 13.6 %collective-permute-start.11 = (bf16[2048,128]{1,0:T(8,128)(2,1)S(1)}, bf16[2048,128]{1,0:T(8,128)(2,1)S(1)}, u32[]{:S(2)}, u32[]{:S(2)}) collective-permute-start(bf16[2048,128]{1,0:T(8,128)(2,1)S(1)} %collective-permute-done.9), channel_id=1, source_target_pairs={{0,15},{1,0},{2,1},{3,2},{4,3},{5,4},{6,5},{7,6},{8,7},{9,8},{10,9... | collective-permute-start | bytes 1572872 | tf_op jit(solution)/shard_map/ppermute | solution.py:21
  101.2 14.5 %collective-permute-start.12 = (bf16[2048,128]{1,0:T(8,128)(2,1)S(1)}, bf16[2048,128]{1,0:T(8,128)(2,1)S(1)}, u32[]{:S(2)}, u32[]{:S(2)}) collective-permute-start(bf16[2048,128]{1,0:T(8,128)(2,1)S(1)} %collective-permute-done.10), channel_id=1, source_target_pairs={{0,1},{1,2},{2,3},{3,4},{4,5},{5,6},{6,7},{7,8},{8,9},{9,10},{10,1... | collective-permute-start | bytes 1572872 | tf_op jit(solution)/shard_map/ppermute | solution.py:18
  106.4 15.3 %collective-permute-start.13 = (bf16[2048,128]{1,0:T(8,128)(2,1)S(1)}, bf16[2048,128]{1,0:T(8,128)(2,1)S(1)}, u32[]{:S(2)}, u32[]{:S(2)}) collective-permute-start(bf16[2048,128]{1,0:T(8,128)(2,1)S(1)} %collective-permute-done.11), channel_id=1, source_target_pairs={{0,15},{1,0},{2,1},{3,2},{4,3},{5,4},{6,5},{7,6},{8,7},{9,8},{10,9... | collective-permute-start | bytes 1572872 | tf_op jit(solution)/shard_map/ppermute | solution.py:21
  115.7 15.7 %collective-permute-start.14 = (bf16[2048,128]{1,0:T(8,128)(2,1)S(1)}, bf16[2048,128]{1,0:T(8,128)(2,1)S(1)}, u32[]{:S(2)}, u32[]{:S(2)}) collective-permute-start(bf16[2048,128]{1,0:T(8,128)(2,1)S(1)} %collective-permute-done.12), channel_id=1, source_target_pairs={{0,1},{1,2},{2,3},{3,4},{4,5},{5,6},{6,7},{7,8},{8,9},{9,10},{10,1... | collective-permute-start | bytes 1572872 | tf_op jit(solution)/shard_map/ppermute | solution.py:18
  208.0 53.8 %copy-start.3 = (f32[2048]{0:T(1024)S(1)}, f32[2048]{0:T(1024)}, u32[]{:S(2)}) copy-start(f32[2048]{0:T(1024)} %param.12) | copy-start | bytes 24580
Sparse Core Ops, SparseCore 0:
  11.1 196.8 all-gather.2
